TPU v7x, 32 devices: a whole 2x2x4 slice. The times are simulated.
32 devices in a mesh: fsdp: 2 (over x), ctx: 4 (over y, core), tp: 4 (over z).
Axes of the slice: x: 2, y: 2, z: 4, core: 2. Of those that a mesh axis runs over, the one named last changes fastest.
Arguments:
- inputs: bfloat16 [4, 16, 196, 768], P('fsdp', 'ctx', 'tp'), may hold values from -6 to 6
- cotangent: bfloat16 [4, 16, 196, 768], P('fsdp', 'ctx', 'tp'), may hold values from -6 to 6
- norm_gain: float32 [3, 768], replicated, may hold values from 0.5 to 1.5
- norm_bias: float32 [3, 768], replicated, may hold values from -1 to 1
- attn_weight: bfloat16 [2, 3, 768, 768], P(None, None, 'fsdp', 'tp'), may hold values from -0.21875 to 0.21875
- attn_bias: float32 [2, 2, 768], P(None, None, 'tp'), may hold values from -1 to 1
- out_weight: bfloat16 [2, 768, 768], P(None, 'tp', 'fsdp'), may hold values from -0.625 to 0.625
- out_bias: float32 [2, 768], replicated, may hold values from -1 to 1
- up_weight: bfloat16 [768, 3072], P('fsdp', 'tp'), may hold values from -0.21875 to 0.21875
- up_bias: float32 [3072], replicated, may hold values from -1 to 1
- down_weight: bfloat16 [3072, 768], P('tp', 'fsdp'), may hold values from -0.109375 to 0.109375
- down_bias: float32 [768], replicated, may hold values from -1 to 1
Outputs:
- outputs: bfloat16 [4, 16, 196, 768], P('fsdp', 'ctx', 'tp')
- input_grad: bfloat16 [4, 16, 196, 768], P('fsdp', 'ctx', 'tp')
- grad_norm_gain: float32 [3, 768], replicated
- grad_norm_bias: float32 [3, 768], replicated
- grad_attn_weight: float32 [2, 3, 768, 768], P(None, None, ('fsdp', 'ctx'), 'tp')
- grad_attn_bias: float32 [2, 2, 768], P(None, None, 'tp')
- grad_out_weight: float32 [2, 768, 768], P(None, 'tp', ('fsdp', 'ctx'))
- grad_out_bias: float32 [2, 768], replicated
- grad_up_weight: float32 [768, 3072], P(('fsdp', 'ctx'), 'tp')
- grad_up_bias: float32 [3072], replicated
- grad_down_weight: float32 [3072, 768], P('tp', ('fsdp', 'ctx'))
- grad_down_bias: float32 [768], replicated
All inputs are finite; a program needn't handle non-finite values.
Results may differ from a plain program's by a relative error of at most 0.025.
Values may be sent and summed in bfloat16 or wider, within the bound.
A program may use at most 128 MiB of HBM per device.

v0:
```python
import jax
import jax.numpy as jnp
from jax import lax
from jax.experimental import pallas as pl
from jax.experimental.pallas import tpu as pltpu
from jax.sharding import PartitionSpec as P

HEAD = 64
EPSILON = 1e-06
BF = jnp.bfloat16
F32 = jnp.float32
MESH = pl.DeviceIdType.MESH
PIECES = 4
ALL = ("fsdp", "ctx", "tp")


def places_of(x, y, k, z):
    return {
        "x": (1 - x, y * 2 + k, z),
        "y": (x, (1 - y) * 2 + k, z),
        "core": (x, y * 2 + 1 - k, z),
        "up": (x, y * 2 + k, z + 1),
        "down": (x, y * 2 + k, z - 1),
        "z1": (x, y * 2 + k, (z // 2) * 2 + 1 - z % 2),
        "z2": (x, y * 2 + k, (z + 2) % 4),
    }


def maybe(when, action):
    if when is None:
        action()
    else:
        pl.when(when)(action)


def gather(shard, bias):
    part = shard.shape[1] // lax.axis_size("ctx")
    mine = lax.dynamic_slice_in_dim(shard, lax.axis_index("ctx") * part, part, 1)
    tall = lax.all_gather(mine, ("fsdp", "ctx"), axis=1, tiled=True)
    return lax.all_gather(tall, "tp", axis=2, tiled=True), lax.all_gather(bias, "tp")


def scatter(grads, vectors):
    tall = lax.psum_scatter(jnp.concatenate(grads), ("fsdp", "ctx"), scatter_dimension=1, tiled=True)
    own = lax.psum_scatter(tall, "tp", scatter_dimension=2, tiled=True)
    return own.astype(F32), lax.psum(vectors, ALL)


def nn(a, b):
    return lax.dot_general(a, b, (((1,), (0,)), ((), ())), preferred_element_type=F32)


def nt(a, b):
    return lax.dot_general(a, b, (((1,), (1,)), ((), ())), preferred_element_type=F32)


def tn(a, b):
    return lax.dot_general(a, b, (((0,), (0,)), ((), ())), preferred_element_type=F32)


def normalise(rows):
    centre = rows - jnp.mean(rows, axis=-1, keepdims=True)
    scale = lax.rsqrt(jnp.mean(centre * centre, axis=-1, keepdims=True) + EPSILON)
    return centre * scale, scale


def chunks(count):
    size = 80 if count % 80 == 0 else 208
    return size, count // size


def norm_into(source, norm, target):
    size, number = chunks(source.shape[0])

    def body(i, carry):
        span = pl.ds(pl.multiple_of(i * size, 16), size)
        unit, _ = normalise(source[span])
        target[span] = (unit * norm[0:1] + norm[1:2]).astype(BF)
        return carry

    lax.fori_loop(0, number, body, 0)


def norm_back_into(source, norm, grad, total, vec, line):
    size, number = chunks(source.shape[0])
    vec[line : line + 2] = jnp.zeros((2, source.shape[1]), F32)

    def body(i, carry):
        span = pl.ds(pl.multiple_of(i * size, 16), size)
        back, gain, shift = norm_back(source[span], norm[0:1], grad[span])
        total[span] += back
        vec[line : line + 1] += gain
        vec[line + 1 : line + 2] += shift
        return carry

    lax.fori_loop(0, number, body, 0)


def round_into(source, target, vec, line):
    size, number = chunks(source.shape[0])
    vec[line : line + 1] = jnp.zeros((1, source.shape[1]), F32)

    def body(i, carry):
        span = pl.ds(pl.multiple_of(i * size, 16), size)
        rounded = source[span].astype(BF)
        target[span] = rounded
        vec[line : line + 1] += jnp.sum(rounded.astype(F32), axis=0, keepdims=True)
        return carry

    lax.fori_loop(0, number, body, 0)


def flip_into(source, target):
    rows = source.shape[0]
    for low in range(0, rows, 128):
        high = min(rows, low + 128)
        target[:, low:high] = source[low:high].T


def norm_back(rows, gain, grad):
    unit, scale = normalise(rows)
    inner = grad * gain
    mean = jnp.mean(inner, axis=-1, keepdims=True)
    along = jnp.mean(inner * unit, axis=-1, keepdims=True)
    return scale * (inner - mean - unit * along), jnp.sum(grad * unit, axis=0, keepdims=True), jnp.sum(
        grad, axis=0, keepdims=True
    )


def lanes_in(low, high):
    lane = lax.broadcasted_iota(jnp.int32, (1, 256), 1)
    return jnp.where((lane >= low) & (lane < high), 1.0, 0.0)


def stack_heads(values):
    return jnp.concatenate(
        [values * lanes_in(i * HEAD, i * HEAD + HEAD).astype(BF) for i in range(3)], axis=0
    )


def pick_heads(stacked):
    rows = stacked.shape[0] // 3
    return sum(
        stacked[i * rows : (i + 1) * rows] * lanes_in(i * HEAD, i * HEAD + HEAD) for i in range(3)
    )


def shifted(values):
    return pltpu.roll(values, 64, axis=1)


def unshifted(values):
    return pltpu.roll(values, 192, axis=1)


def block(w_ref, t, start, size):
    return w_ref[:, pl.ds(pl.multiple_of(t * (w_ref.shape[1] // 4) + start, 128), size)]


def spatial_probs(ref):
    return lambda t, g: ref.at[t, g]


def small_probs(ref, size):
    def find(t, g):
        row, lane = ((g % 2) * 3 * size, 0) if g < 4 else (0, 128)
        return ref.at[t, g // 2 % 2, pl.ds(row, 3 * size), pl.ds(lane, size)]

    return find


class Attention:
    def __init__(self, groups, rows, penalty, w, bias, q, k, v, o, p):
        self.groups, self.rows, self.penalty = groups, rows, penalty
        self.w, self.bias, self.q, self.k, self.v, self.o, self.p = w, bias, q, k, v, o, p

    def spans(self):
        return [(g, pl.ds(g * self.rows, self.rows)) for g in range(self.groups)]

    def forward(self, normed, total, after=lambda i: None):
        used = lanes_in(0, 192)

        def body(t, carry):
            mixed = nn(normed[...], block(self.w, t, 0, 640))
            self.q[t] = ((mixed[:, :256] + self.bias[t, 0:1]) * used).astype(BF)
            self.k[t] = (unshifted(mixed[:, 128:384]) * used).astype(BF)
            self.v[t] = ((mixed[:, 384:] + self.bias[t, 1:2]) * used).astype(BF)
            for g, span in self.spans():
                scores = nt(stack_heads(self.q[t, span]), self.k[t, span]) * 0.125 + self.penalty()
                weights = jnp.exp(scores - jnp.max(scores, axis=-1, keepdims=True))
                weights = weights * (1.0 / jnp.sum(weights, axis=-1, keepdims=True))
                weights = weights.astype(BF)
                self.p(t, g)[...] = weights
                out = pick_heads(nn(weights, self.v[t, span]))
                self.o[t, span] = shifted(out).astype(BF)
            total[...] += nt(self.o[t, pl.ds(0, self.groups * self.rows)], block(self.w, t, 512, 256))
            after(t)
            return carry

        lax.fori_loop(0, 4, body, 0)

    def backward(self, normed_t, branch, branch_t, dk, dv, grad_normed, grad_w, grad_bias, after):
        used = lanes_in(0, 192)

        def body(i, carry):
            t = (3 * i) % 4
            grad_o = (unshifted(nn(branch[...], block(self.w, t, 512, 256))) * used).astype(BF)
            dq = []
            for g, span in self.spans():
                stacked = stack_heads(grad_o[g * self.rows : (g + 1) * self.rows])
                weights = self.p(t, g)[...]
                probs = weights.astype(F32)
                grad_p = nt(stacked, self.v[t, span])
                inner = jnp.sum(probs * grad_p, axis=-1, keepdims=True)
                grad_s = (probs * (grad_p - inner)).astype(BF)
                dq.append((pick_heads(nn(grad_s, self.k[t, span])) * 0.125).astype(BF))
                dk[span] = shifted(tn(grad_s, stack_heads(self.q[t, span])) * 0.125).astype(BF)
                dv[span] = tn(weights, stacked).astype(BF)
            extra = normed_t.shape[1] - self.groups * self.rows
            if extra:
                dq.append(jnp.zeros((extra, 256), BF))
            dq = jnp.concatenate(dq, axis=0)
            grad_normed[...] += (
                nt(dq, block(self.w, t, 0, 256))
                + nt(dk[...], block(self.w, t, 128, 256))
                + nt(dv[...], block(self.w, t, 384, 256))
            )
            for start, low, high in (
                (0, nn(normed_t[...], dq), nn(normed_t[...], dk[...])),
                (384, nn(normed_t[...], dv[...]), nn(branch_t[...], self.o[t])),
            ):
                columns = pl.multiple_of(t * (self.w.shape[1] // 4) + start, 128)
                grad_w[:, pl.ds(columns, 128)] = low[:, :128].astype(BF)
                grad_w[:, pl.ds(columns + 128, 128)] = (low[:, 128:] + high[:, :128]).astype(BF)
                grad_w[:, pl.ds(columns + 256, 128)] = high[:, 128:].astype(BF)
            grad_bias[t, 0:1] = jnp.sum(dq.astype(F32), axis=0, keepdims=True)
            grad_bias[t, 1:2] = jnp.sum(dv[...].astype(F32), axis=0, keepdims=True)
            after(i)
            return carry

        lax.fori_loop(0, 4, body, 0)


SP = 208


def spatial_penalty(places):
    def penalty():
        lane = lax.broadcasted_iota(jnp.int32, (1, SP), 1)
        return jnp.where(lane < places, 0.0, -1e30)
    return penalty


def spatial_forward_kernel(x_ref, w_ref, bias_ref, norm_ref, ob_ref, h_out, q, k, v, o, p, total, normed):
    clips, places, model = x_ref.shape
    for g in range(clips):
        total[pl.ds(g * SP, places)] = x_ref[g].astype(F32)
        total[pl.ds(g * SP + places, SP - places)] = jnp.zeros((SP - places, model), F32)
        span = pl.ds(g * SP, SP)
        unit, _ = normalise(total[span])
        normed[span] = (unit * norm_ref[0:1] + norm_ref[1:2]).astype(BF)
        total[span] += ob_ref[...]
    att = Attention(clips, SP, spatial_penalty(places), w_ref.at[0], bias_ref, q, k, v, o, spatial_probs(p))
    att.forward(normed, total)
    for g in range(clips):
        h_out[g] = total[pl.ds(g * SP, places)].astype(BF)


def spatial_back_kernel(x_ref, g_ref, w_ref, norm_ref, q, k, v, o, p,
                        gx_out, gw, gbias, gvec, total, normed, normed_t, branch, branch_t, dk, dv, gn, rows_in):
    clips, places, model = x_ref.shape
    for g in range(clips):
        for ref, source in ((rows_in, x_ref), (total, g_ref)):
            ref[pl.ds(g * SP, places)] = source[g].astype(F32)
            ref[pl.ds(g * SP + places, SP - places)] = jnp.zeros((SP - places, model), F32)
    attention_back(Attention(clips, SP, None, w_ref.at[0], None, q, k, v, o, spatial_probs(p)),
                   rows_in, total, norm_ref, normed, normed_t, branch, branch_t, dk, dv, gn, gw.at[0], gbias, gvec, 0, lambda i: None)
    for g in range(clips):
        gx_out[g] = total[pl.ds(g * SP, places)].astype(BF)


def attention_back(
    att, rows_in, total, norm, normed, normed_t, branch, branch_t, dk, dv, gn, grad_w, gbias, vec, line, after
):
    round_into(total, branch, vec, line + 2)
    flip_into(branch, branch_t)
    norm_into(rows_in, norm, normed)
    flip_into(normed, normed_t)
    gn[...] = jnp.zeros(gn.shape, F32)
    att.backward(normed_t, branch, branch_t, dk, dv, gn, grad_w, gbias, after)
    norm_back_into(rows_in, norm, gn, total, vec, line)


def by_pair(source, target, mix):
    frames, pairs, model = source.shape
    for f in range(frames):
        values = source[f].astype(F32)
        for i in range(model // 128):
            mix[i, pl.ds(f, pairs, stride=frames)] = values[:, i * 128 : i * 128 + 128]
    for i in range(model // 128):
        target[:, i * 128 : i * 128 + 128] = mix[i]


def by_frame(source, target, mix):
    frames, pairs, model = target.shape
    for i in range(model // 128):
        mix[i] = source[:, i * 128 : i * 128 + 128]
    for f in range(frames):
        for i in range(model // 128):
            target[f, :, i * 128 : i * 128 + 128] = mix[i, pl.ds(f, pairs, stride=frames)].astype(BF)


TG = 5


def temporal_kernel(h_ref, g_ref, w_ref, u_ref, d_ref, bias_ref, norm_ref, norm2_ref, ob_ref, ub_ref, db_ref, pen_ref,
                    y_out, g_out, gw, gu, gd, gbias, gvec, gvec2, gub,
                    q, k, v, o, p, rows_in, total, third, grad, normed, normed_t, branch, branch_t, dk, dv, gn, mix):
    frames, pairs, model = h_ref.shape
    rows = frames * pairs
    by_pair(h_ref, rows_in, mix)
    by_pair(g_ref, grad, mix)
    unit, _ = normalise(rows_in[...])
    normed[...] = (unit * norm_ref[0:1] + norm_ref[1:2]).astype(BF)
    third[...] = rows_in[...] + ob_ref[...]
    group = TG * frames
    att = Attention(pairs // TG, group, lambda: pen_ref[...], w_ref.at[0], bias_ref, q, k, v, o, spatial_probs(p))
    att.forward(normed, third)
    unit, _ = normalise(third[...])
    n2 = unit * norm2_ref[0:1] + norm2_ref[1:2]
    normed[...] = n2.astype(BF)
    normed_t[...] = n2.T.astype(BF)
    branch[...] = grad[...].astype(BF)
    branch_t[...] = grad[...].T.astype(BF)
    gvec2[2:3] = jnp.sum(grad[...], axis=0, keepdims=True)
    total[...] = third[...] + db_ref[...]
    gn[...] = jnp.zeros_like(gn)
    size = 384
    def mlp(j, carry):
        columns = pl.ds(pl.multiple_of(j * size, 128), size)
        up = u_ref[0, :, columns]
        down = d_ref[0, :, columns]
        hidden = nn(normed[...], up) + ub_ref[j]
        half = 0.5 + 0.5 * lax.erf(hidden * (2.0 ** -0.5))
        active = (hidden * half).astype(BF)
        slope = half + hidden * (jnp.exp(-0.5 * hidden * hidden) * ((2.0 * jnp.pi) ** -0.5))
        grad_hidden = nn(branch[...], down) * slope
        rounded = grad_hidden.astype(BF)
        gub[j] = jnp.sum(rounded.astype(F32), axis=0, keepdims=True)
        total[...] += nt(active, down)
        gn[...] += nt(rounded, up)
        gd[0, :, columns] = nn(branch_t[...], active).astype(BF)
        gu[0, :, columns] = nn(normed_t[...], rounded).astype(BF)
        return carry
    lax.fori_loop(0, u_ref.shape[2] // size, mlp, 0)
    by_frame(total, y_out, mix)
    back, gain, shift = norm_back(third[...], norm2_ref[0:1], gn[...])
    grad[...] += back
    gvec2[0:1] = gain
    gvec2[1:2] = shift
    attention_back(att, rows_in, grad, norm_ref, normed, normed_t, branch, branch_t, dk, dv, gn, gw.at[0], gbias, gvec, 0, lambda i: None)
    by_frame(grad, g_out, mix)


def piece_spec(piece, whole):
    return pl.BlockSpec((1,) + whole.shape[1:], lambda i: (piece, 0, 0))


def full_spec(value):
    return pl.BlockSpec(value.shape, lambda i: (0,) * len(value.shape))


def run(kernel, args, specs, outs, scratch, name):
    return pl.pallas_call(
        kernel, grid=(1,),
        out_shape=outs, in_specs=specs, out_specs=[full_spec(out) for out in outs], scratch_shapes=scratch,
        compiler_params=pltpu.CompilerParams(vmem_limit_bytes=63 * 2**20),
        name=name,
    )(*args)


def shape(*size, dtype=BF):
    return jax.ShapeDtypeStruct(size, dtype)


def spatial_forward(x, whole, bias, norm, out_bias):
    clips, places, model = x.shape
    rows = clips * SP
    args = (x, whole, bias, norm, out_bias)
    specs = [full_spec(a) for a in args]
    specs[1] = piece_spec(0, whole)
    outs = [shape(clips, places, model)] + [shape(4, rows, 256)] * 4 + [shape(4, clips, 3 * SP, SP)]
    return run(spatial_forward_kernel, args, specs, outs,
               [pltpu.VMEM((rows, model), F32), pltpu.VMEM((rows, model), BF)], "spatial_forward")


def spatial_back(x, g, whole, norm, kept):
    clips, places, model = x.shape
    rows = clips * SP
    args = (x, g, whole, norm) + tuple(kept)
    specs = [full_spec(a) for a in args]
    specs[2] = piece_spec(0, whole)
    outs = [shape(clips, places, model), shape(1, *whole.shape[1:]), shape(4, 2, 256, dtype=F32), shape(3, model, dtype=F32)]
    scratch = [pltpu.VMEM((rows, model), F32), pltpu.VMEM((rows, model), BF), pltpu.VMEM((model, rows), BF), pltpu.VMEM((rows, model), BF),
               pltpu.VMEM((model, rows), BF), pltpu.VMEM((rows, 256), BF), pltpu.VMEM((rows, 256), BF),
               pltpu.VMEM((rows, model), F32), pltpu.VMEM((rows, model), F32)]
    return run(spatial_back_kernel, args, specs, outs, scratch, "spatial_back")


def temporal(h, g, whole, bias, norm, norm2, out_bias, up_bias, down_bias):
    frames, pairs, model = h.shape
    rows = frames * pairs
    group = TG * frames
    row = jnp.arange(3 * group)[:, None] % group // frames
    column = jnp.arange(group)[None] // frames
    penalty = jnp.where(row == column, 0.0, -1e30).astype(F32)
    args = (h, g, whole, whole, whole, bias, norm, norm2, out_bias, up_bias.reshape(-1, 1, 384), down_bias, penalty)
    specs = [full_spec(a) for a in args]
    for i, piece in ((2, 1), (3, 2), (4, 3)):
        specs[i] = piece_spec(piece, whole)
    hidden = whole.shape[2]
    outs = [shape(frames, pairs, model), shape(frames, pairs, model), shape(1, model, hidden), shape(1, model, hidden),
            shape(1, model, hidden), shape(4, 2, 256, dtype=F32), shape(3, model, dtype=F32), shape(3, model, dtype=F32),
            shape(hidden // 384, 1, 384, dtype=F32)]
    big = pltpu.VMEM((rows, model), F32)
    low = pltpu.VMEM((rows, model), BF)
    flip = pltpu.VMEM((model, rows), BF)
    part = pltpu.VMEM((rows, 256), BF)
    scratch = [pltpu.VMEM((4, rows, 256), BF)] * 4 + [pltpu.VMEM((4, pairs // TG, 3 * group, group), BF)] + [
        big, big, big, big, low, flip, low, flip, part, part, big, pltpu.VMEM((model // 128, rows, 128), F32)]
    return run(temporal_kernel, args, specs, outs, scratch, "temporal_and_mlp")


STEPS = 16


class Refs:
    def __init__(self, names, refs):
        for name, ref in zip(names, refs, strict=True):
            setattr(self, name, ref)


def pair_segments(index, share, clips, places):
    found = []
    for clip in range(clips):
        low = max(index * share, clip * places)
        high = min(index * share + share, clip * places + places)
        if low < high:
            found.append((low - index * share, high - low, clip, low - clip * places))
    return found


class Reduction:
    def __init__(self, r, places, x, y, k, z, rows, width):
        self.r, self.places, self.rows, self.width = r, places, rows, width
        self.x, self.y, self.k, self.z = x, y, k, z
        self.quads = [(f, yy) for f in range(2) for yy in range(2)]
        self.last = 3

    def piece_of(self, s):
        if isinstance(s, int):
            return 2 + s % 2 if s < 8 else 1 if s < 12 else 0
        early, middle = (s < 8).astype(jnp.int32), ((s >= 8) & (s < 12)).astype(jnp.int32)
        return early * (2 + s % 2) + middle

    def tp_of(self, s):
        if isinstance(s, int):
            return 3 * (s // 2 if s < 8 else s) % 4
        early = (s < 8).astype(jnp.int32)
        return (3 * (early * (s // 2) + (1 - early) * s)) % 4

    def spot(self, f, yy, kk, s):
        row = pl.multiple_of((f * 4 + yy * 2 + kk) * self.rows, 16)
        column = pl.multiple_of(self.tp_of(s) * self.width, 128)
        return self.r.w.at[self.piece_of(s), pl.ds(row, self.rows), pl.ds(column, self.width)]

    def remote(self, src, dst, send, recv, side):
        return pltpu.make_async_remote_copy(
            src_ref=src, dst_ref=dst, send_sem=send, recv_sem=recv,
            device_id=self.places[side], device_id_type=MESH,
        )

    def core_copy(self, s, f, yy):
        r = self.r
        return self.remote(
            self.spot(f, yy, 1 - self.k, s), r.r1.at[s, f, yy], r.s1.at[s, f, yy], r.q1s.at[s, f, yy], "core"
        )

    def diag_copy(self, s, side):
        r = self.r
        return self.remote(r.r1.at[s, 1 - self.x, 1 - self.y], r.r2.at[s], r.s2.at[s], r.q2.at[s], side)

    def x_copy(self, s):
        r = self.r
        return self.remote(r.r1.at[s, 1 - self.x, self.y], r.r3x.at[s], r.s3x.at[s], r.q3x.at[s], "x")

    def y_copy(self, s):
        r = self.r
        return self.remote(r.r1.at[s, self.x, 1 - self.y], r.r3y.at[s], r.s3y.at[s], r.q3y.at[s], "y")

    def up_copy(self, s):
        r = self.r
        return self.remote(r.r1.at[s, self.x, self.y], r.rz.at[s], r.sz.at[s], r.qup.at[s], "up")

    def down_copy(self, s, owner=False):
        r = self.r
        target = r.re.at[self.piece_of(s)] if owner else r.rz.at[s]
        return self.remote(r.r1.at[s, self.x, self.y], target, r.sz.at[s], r.qdn.at[s], "down")

    def start(self, s):
        for f, yy in self.quads:
            self.core_copy(s, f, yy).start()

    def even_odd(self, s, even, odd):
        if isinstance(s, int):
            (odd if s % 2 else even)()
        else:
            pl.when(s % 2 == 0)(even)
            pl.when(s % 2 == 1)(odd)

    def chip_sum(self, s):
        r1 = self.r.r1
        for f, yy in self.quads:
            self.core_copy(s, f, yy).wait_recv()
            r1[s, f, yy] = r1[s, f, yy] + self.spot(f, yy, self.k, s)[...]

        def even():
            self.diag_copy(s, "x").start()
            self.x_copy(s).start()

        def odd():
            self.diag_copy(s, "y").start()
            self.y_copy(s).start()

        self.even_odd(s, even, odd)

    def turn(self, s):
        r1, r2, x, y = self.r.r1, self.r.r2, self.x, self.y
        self.diag_copy(s, "x").wait_recv()

        def even():
            r1[s, x, 1 - y] = r1[s, x, 1 - y] + r2[s]
            self.y_copy(s).start()

        def odd():
            r1[s, 1 - x, y] = r1[s, 1 - x, y] + r2[s]
            self.x_copy(s).start()

        self.even_odd(s, even, odd)

    def plane_sum(self, s):
        r = self.r
        self.x_copy(s).wait_recv()
        self.y_copy(s).wait_recv()
        total = r.r1[s, self.x, self.y].astype(F32) + r.r3x[s].astype(F32) + r.r3y[s].astype(F32)
        r.r1[s, self.x, self.y] = total.astype(BF)

    def line(self, s, hop):
        r, x, y, z, last = self.r, self.x, self.y, self.z, self.last
        t = self.tp_of(s)

        @pl.when((z < t) & (z == hop))
        def _():
            if hop > 0:
                self.up_copy(s).wait_recv()
                r.r1[s, x, y] = r.r1[s, x, y] + r.rz[s]
            self.up_copy(s).start()

        @pl.when((z > t) & (last - z == hop))
        def _():
            if hop > 0:
                self.down_copy(s).wait_recv()
                r.r1[s, x, y] = r.r1[s, x, y] + r.rz[s]

            @pl.when(z - 1 == t)
            def _():
                self.down_copy(s, True).start()

            @pl.when(z - 1 != t)
            def _():
                self.down_copy(s).start()

        far = z + (last - 2 * z) * ((last - 2 * z) > 0).astype(jnp.int32)

        @pl.when((z == t) & (far == hop))
        def _():
            piece = self.piece_of(s)
            r.own[piece] = r.r1[s, x, y].astype(F32)

            @pl.when(z > 0)
            def _():
                self.up_copy(s).wait_recv()
                r.own[piece] = r.own[piece] + r.rz[s].astype(F32)

            @pl.when(z < last)
            def _():
                self.down_copy(s, True).wait_recv()
                r.own[piece] = r.own[piece] + r.re[piece].astype(F32)

    def guard(self, action, s, *rest):
        if isinstance(s, int):
            if 0 <= s < STEPS:
                action(s, *rest)
        else:

            @pl.when((s >= 0) & (s < STEPS))
            def _():
                action(s, *rest)

    def tick(self, n):
        self.guard(self.chip_sum, n - 1)
        self.guard(self.turn, n - 3)
        self.guard(self.plane_sum, n - 5)
        for hop in range(4):
            self.guard(self.line, n - 7 - 2 * hop, hop)

    def finish(self):
        def body(s, carry):
            for f, yy in self.quads:
                self.core_copy(s, f, yy).wait_send()
            self.diag_copy(s, "x").wait_send()
            self.x_copy(s).wait_send()
            self.y_copy(s).wait_send()

            @pl.when(self.z != self.tp_of(s))
            def _():
                self.up_copy(s).wait_send()

            return carry

        lax.fori_loop(0, STEPS, body, 0)


STAGES = 7
X_LAST = (3,)
FIRST = [[(0, 0), (1, 0)], [(0, 1)], [(0, 2), (1, 1)], [(0, 3), (1, 2), (2, 0), (0, 4), (1, 3), (3, 0), (0, 5), (1, 4), (2, 1), (0, 6)]]
WITH_SPATIAL = [[(1, 5)], [(3, 1)], [(1, 6)], [(2, 2)]]
WITH_EXCHANGE = [[(3, 2)], [(2, 3)], [(3, 3)]]
WITH_TEMPORAL = [[(2, 4)], [(3, 4)], [(2, 5)], [(3, 5)]]
AT_END = [(2, 6), (3, 6)]


class Gather:
    def __init__(self, r, places, x, y, k, z):
        self.r, self.places, self.x, self.k, self.z = r, places, x, k, z
        self.c = y * 2 + k
        self.rows, self.width = r.shard.shape[1] // 4, r.shard.shape[2]
        self.sends = []
        c, other_y, last = self.c, (1 - y) * 2 + k, 3
        self.stages = [[] for _ in range(STAGES)]

        def wait(stage, unit, when=None):
            self.stages[stage].append(("wait", unit, when))

        def send(stage, side, unit, when=None, mine=False, x_last=None):
            entry = (side, unit, when, mine, x_last, len(self.sends))
            self.sends.append(entry)
            self.stages[stage].append(("send",) + entry)

        me = (x, c, z)
        send(0, "up", me, z < last, True)
        send(0, "down", me, z > 0, True)
        send(0, "x", me, None, True)
        send(0, "x", (x, other_y, z), None, True)
        for d in (1, 2, 3):
            for sign in (-1, 1):
                t = z + sign * d
                have = (t >= 0) if sign < 0 else (t <= last)
                unit = (x, c, t)
                wait(d, unit, have)
                if d < last:
                    if sign < 0:
                        send(d, "up", unit, have & (z < last))
                    else:
                        send(d, "down", unit, have & (z > 0))
                for side in ("x", "y", "core"):
                    send(d, side, unit, have)
            if d == 1:
                wait(1, (1 - x, c, z))
                send(1, "core", (1 - x, c, z))
            if d == 2:
                wait(2, (1 - x, other_y, z))
                send(2, "core", (1 - x, other_y, z))
        for d in (1, 2, 3):
            for sign in (-1, 1):
                t = z + sign * d
                have = (t >= 0) if sign < 0 else (t <= last)
                wait(d + 1, (1 - x, c, t), have)
                send(d + 1, "y", (1 - x, c, t), have, x_last=False)
                send(d + 1, "core", (1 - x, c, t), have)
                wait(d + 1, (x, other_y, t), have)
                send(d + 1, "x", (x, other_y, t), have, x_last=True)
                send(d + 1, "core", (x, other_y, t), have)
                wait(d + 2, (1 - x, other_y, t), have)
                send(d + 2, "core", (1 - x, other_y, t), have)
                for f in (x, 1 - x):
                    for yy in (y, 1 - y):
                        wait(6, (f, yy * 2 + 1 - k, t), have)
        for yy in (y, 1 - y):
            wait(6, (1 - x, yy * 2 + 1 - k, z))

    def spot(self, piece, unit):
        f, cc, t = unit
        row = pl.multiple_of((f * 4 + cc) * self.rows, 16)
        return self.r.w.at[piece, pl.ds(row, self.rows), pl.ds(pl.multiple_of(t * self.width, 128), self.width)]

    def active(self, piece):
        return lambda entry: entry[4] is None or entry[4] == (piece in X_LAST)

    def copy(self, piece, entry):
        side, unit, _, mine, _, number = entry
        f, cc, t = unit
        target = self.spot(piece, unit)
        source = self.r.shard.at[piece, pl.ds(pl.multiple_of(cc * self.rows, 16), self.rows)] if mine else target
        return pltpu.make_async_remote_copy(
            src_ref=source, dst_ref=target,
            send_sem=self.r.ws.at[number, piece], recv_sem=self.r.wq.at[(f * 4 + cc) * 4 + t, piece],
            device_id=self.places[side], device_id_type=MESH,
        )

    def own(self, piece):
        row = pl.multiple_of(self.x * self.rows * 4, 16)
        column = pl.multiple_of(self.z * self.width, 128)
        target = self.r.w.at[piece, pl.ds(row, self.rows * 4), pl.ds(column, self.width)]
        return pltpu.make_async_copy(self.r.shard.at[piece], target, self.r.wl.at[piece])

    def put(self, piece):
        return pltpu.make_async_copy(self.r.w.at[piece], self.r.whole.at[piece], self.r.wo.at[piece])

    def arrived(self, piece, unit):
        f, cc, t = unit
        ref = self.spot(piece, unit)
        pltpu.make_async_copy(ref, ref, self.r.wq.at[(f * 4 + cc) * 4 + t, piece]).wait()

    def stage(self, piece, number):
        if number == 0:
            self.own(piece).start()
        for kind, *rest in self.stages[number]:
            if kind == "wait":
                unit, when = rest
                maybe(when, lambda: self.arrived(piece, unit))
            elif self.active(piece)(rest):
                maybe(rest[2], lambda: self.copy(piece, rest).start())
        if number == STAGES - 1:
            self.own(piece).wait()
            self.put(piece).start()

    def run(self, items):
        for piece, number in items:
            self.stage(piece, number)

    def beside(self, plan):
        def after(i):
            for step, items in enumerate(plan):
                pl.when(i == step)(lambda: self.run(items))

        return after

    def finish(self):
        always = [entry for entry in self.sends if entry[4] is None]

        def body(piece, carry):
            for entry in always:
                maybe(entry[2], lambda: self.copy(piece, entry).wait_send())
            self.put(piece).wait()
            return carry

        lax.fori_loop(0, PIECES, body, 0)
        for piece in range(PIECES):
            for entry in self.sends:
                if entry[4] is not None and self.active(piece)(entry):
                    maybe(entry[2], lambda: self.copy(piece, entry).wait_send())


FORWARD_NAMES = [
    "shard", "bias", "x_in", "g_in", "norm", "ob", "penalty",
    "whole", "x_out", "q0", "k0", "v0", "o0", "p0", "q1", "k1", "v1", "o1", "p1", "rows_out", "third_out", "grad_out",
    "w", "bias_all", "q", "k", "v", "o", "p", "total", "normed", "rows_in", "third", "grad", "mix",
    "x_recv", "g_send", "g_recv", "h_send", "h_recv",
    "ws", "wq", "wl", "wo", "bs", "bq", "xs", "xq", "cs", "cq", "hs", "hq", "keep",
]


def forward_kernel(*refs):
    r = Refs(FORWARD_NAMES, refs)
    x, c, z = lax.axis_index("fsdp"), lax.axis_index("ctx"), lax.axis_index("tp")
    y, k = c // 2, c % 2
    clips, home_places = r.x_in.shape[0], r.x_in.shape[2]
    model = r.x_in.shape[3]
    places = home_places * 4
    frames, share = r.h_recv.shape[:2]
    rows = frames * share
    me = c * 4 + z
    where = places_of(x, y, k, z)

    barrier = pltpu.get_barrier_semaphore()
    pl.semaphore_signal(barrier, inc=1, device_id=where["x"], device_id_type=MESH)

    def greet(d, carry):
        peer = (me + d) % 16
        pl.semaphore_signal(barrier, inc=1, device_id=(x, peer // 4, peer % 4), device_id_type=MESH)
        return carry

    lax.fori_loop(1, 16, greet, 0)
    pl.semaphore_wait(barrier, 16)

    def remote(src, dst, send, recv, place):
        return pltpu.make_async_remote_copy(
            src_ref=src, dst_ref=dst, send_sem=send, recv_sem=recv, device_id=place, device_id_type=MESH
        )

    gather = Gather(r, where, x, y, k, z)
    early = []
    for d in range(1, 4):
        to = (z + d) % 4
        place = (x, c, to)
        early.append(remote(r.x_in.at[:, to], r.x_recv.at[z], r.xs.at[d], r.xq.at[d], place))
        early.append(remote(r.bias, r.bias_all.at[z], r.bs.at[d], r.bq.at[d], place))
    early.append(pltpu.make_async_copy(r.x_in.at[:, z], r.x_recv.at[z], r.xs.at[0]))
    early.append(pltpu.make_async_copy(r.bias, r.bias_all.at[z], r.bs.at[0]))
    for copy in early:
        copy.start()
    gather.run(FIRST[0])

    def share_out(f, carry):
        for clip in range(clips):
            r.third[64 * clip + 64 : 64 * clip + 64 + home_places] = r.g_in[clip, f].astype(F32)
        for to in range(4):
            used = 0
            for start, count, clip, place in pair_segments(to, share, clips, home_places):
                low = 64 * clip + 64 + place
                r.third[start : start + count] = r.third[low : low + count]
                used = start + count
            if used < share:
                r.third[used:share] = jnp.zeros((share - used, model), F32)
            r.g_send[to * 4 + f] = r.third[0:share].astype(BF)
        return carry

    lax.fori_loop(0, 4, share_out, 0)
    gather.run(FIRST[1])
    shares = []
    for d in range(1, 4):
        to = (c + d) % 4
        shares.append(
            remote(r.g_send.at[pl.ds(to * 4, 4)], r.g_recv.at[pl.ds(c * 4, 4)], r.cs.at[d], r.cq.at[d], (x, to, z))
        )
    shares.append(
        pltpu.make_async_copy(r.g_send.at[pl.ds(c * 4, 4)], r.g_recv.at[pl.ds(c * 4, 4)], r.cs.at[0])
    )
    for copy in shares:
        copy.start()
    gather.run(FIRST[2])

    for copy in early:
        copy.wait()
    keep_x = pltpu.make_async_copy(r.x_recv, r.x_out, r.keep.at[0])
    keep_x.start()
    for clip in range(clips):
        for zz in range(4):
            row = clip * SP + zz * home_places
            r.total[row : row + home_places] = r.x_recv[zz, clip].astype(F32)
        r.total[clip * SP + places : clip * SP + SP] = jnp.zeros((SP - places, model), F32)
    norm_into(r.total, r.norm.at[0], r.normed)
    r.total[...] += r.ob[0:1]
    gather.run(FIRST[3])
    att = Attention(clips, SP, spatial_penalty(places), r.w.at[0], r.bias_all.at[:, 0], r.q, r.k, r.v, r.o, spatial_probs(r.p))
    att.forward(r.normed, r.total, gather.beside(WITH_SPATIAL))
    values = (r.q, r.k, r.v, r.o, r.p)
    kept = [
        pltpu.make_async_copy(source, target, r.keep.at[1 + i])
        for i, (source, target) in enumerate(zip(values, (r.q0, r.k0, r.v0, r.o0, r.p0)))
    ]
    for copy in kept:
        copy.start()
    for cc in range(4):
        for zz in range(4):
            used = 0
            for start, count, clip, place in pair_segments(cc, share, clips, home_places):
                row = clip * SP + zz * home_places + place
                r.third[start : start + count] = r.total[row : row + count]
                used = start + count
            if used < share:
                r.third[used:share] = jnp.zeros((share - used, model), F32)
            r.h_send[cc * 4 + zz] = r.third[0:share].astype(BF)

    def to_column(d):
        peer = (me + d) % 16
        return remote(
            r.h_send.at[peer], r.h_recv.at[me], r.hs.at[d], r.hq.at[d], (x, peer // 4, peer % 4)
        )

    def go(d, carry):
        to_column(d).start()
        return carry

    lax.fori_loop(1, 16, go, 0)
    r.h_recv[me] = r.h_send[me]
    for copy in shares:
        copy.wait()
    gather.run(WITH_EXCHANGE[0])
    by_pair(r.g_recv, r.grad, r.mix)
    gather.run(WITH_EXCHANGE[1])

    def come(d, carry):
        to_column(d).wait()
        return carry

    lax.fori_loop(1, 16, come, 0)

    by_pair(r.h_recv, r.rows_in, r.mix)
    normed = r.normed.at[pl.ds(0, rows)]
    norm_into(r.rows_in, r.norm.at[1], normed)
    r.third[...] = r.rows_in[...] + r.ob[1:2]
    for copy in kept:
        copy.wait()
    group = TG * frames
    att = Attention(
        share // TG, group, lambda: r.penalty[...], r.w.at[1], r.bias_all.at[:, 1],
        *(ref.at[:, pl.ds(0, rows)] for ref in (r.q, r.k, r.v)), r.o, small_probs(r.p, group),
    )
    gather.run(WITH_EXCHANGE[2])
    att.forward(normed, r.third, gather.beside(WITH_TEMPORAL))
    gather.run(AT_END)
    kept = [
        pltpu.make_async_copy(source, target, r.keep.at[1 + i])
        for i, (source, target) in enumerate(
            zip(
                values + (r.rows_in, r.third, r.grad),
                (r.q1, r.k1, r.v1, r.o1, r.p1, r.rows_out, r.third_out, r.grad_out),
            )
        )
    ]
    for copy in kept:
        copy.start()
    gather.finish()
    for copy in kept:
        copy.wait()
    keep_x.wait()


def whole_penalty(group, frames):
    row = jnp.arange(3 * group)[:, None] % group // frames
    column = jnp.arange(group)[None] // frames
    return jnp.where(row == column, 0.0, -1e30).astype(F32)


def forward(shard, bias, inputs, cotangent, norm, out_bias, frames, share):
    clips, _, home_places, model = inputs.shape
    rows, srows = frames * share, clips * SP
    args = (shard, bias, inputs, cotangent, norm, out_bias, whole_penalty(TG * frames, frames))
    anywhere, vmem = pl.BlockSpec(memory_space=pl.ANY), pl.BlockSpec(memory_space=pltpu.VMEM)
    whole = (PIECES, shard.shape[1] * 2, shard.shape[2] * 4)
    blocks = (4, clips, home_places, model)
    part, probs = (4, srows, 256), (4, clips, 3 * SP, SP)
    attention = [part] * 4 + [probs]
    outs = [shape(*whole), shape(*blocks)] + [shape(*size) for size in attention * 2]
    outs += [shape(rows, model, dtype=F32)] * 3
    dma = pltpu.SemaphoreType.DMA
    sends = 58
    scratch = (
        [pltpu.VMEM(whole, BF), pltpu.VMEM((4,) + bias.shape, F32)]
        + [pltpu.VMEM(size, BF) for size in attention]
        + [pltpu.VMEM((srows, model), F32), pltpu.VMEM((srows, model), BF)]
        + [pltpu.VMEM((rows, model), F32)] * 3
        + [pltpu.VMEM((model // 128, rows, 128), F32), pltpu.VMEM(blocks, BF)]
        + [pltpu.VMEM((frames, share, model), BF)] * 4
        + [dma((sends, PIECES)), dma((32, PIECES)), dma((PIECES,)), dma((PIECES,))]
        + [dma((4,))] * 6
        + [dma((16,))] * 2
        + [dma((9,))]
    )
    return pl.pallas_call(
        forward_kernel,
        out_shape=outs,
        in_specs=[vmem, vmem, anywhere, vmem, vmem, vmem, vmem],
        out_specs=[anywhere] * len(outs),
        scratch_shapes=scratch,
        compiler_params=pltpu.CompilerParams(
            collective_id=0, has_side_effects=True, vmem_limit_bytes=67043328
        ),
        name="forward",
    )(*args)


BACK_NAMES = [
    "x", "rows_from", "third_from", "grad_from", "whole", "q1", "k1", "v1", "o1", "p1", "q0", "k0", "v0", "o0", "p0",
    "norm", "ub", "db", "y_home", "g_home", "own", "vectors", "w", "q", "k", "v", "o", "p", "rows_in", "total",
    "third", "grad", "gn", "mix", "normed", "normed_t", "branch", "branch_t", "dk", "dv", "y_send",
    "g_send", "g_recv", "home_send", "bias1", "bias0", "ups", "r1", "r2", "r3x", "r3y", "rz", "re", "va",
    "vr", "load", "s1", "q1s", "s2", "q2", "s3x", "s3y", "q3x", "q3y", "sz", "qup", "qdn", "vs", "vq", "ys",
    "yq", "gs", "gq", "hs", "hq", "keep", "early",
]


def back_kernel(*refs):
    r = Refs(BACK_NAMES, refs)
    x, c, z = lax.axis_index("fsdp"), lax.axis_index("ctx"), lax.axis_index("tp")
    y, k = c // 2, c % 2
    _, clips, home_places, model = r.x.shape
    frames, share = r.y_send.shape[:2]
    rows = frames * share
    places = home_places * 4
    me = c * 4 + z
    where = places_of(x, y, k, z)

    barrier = pltpu.get_barrier_semaphore()
    pl.semaphore_signal(barrier, inc=1, device_id=where["x"], device_id_type=MESH)

    def greet(d, carry):
        peer = (me + d) % 16
        pl.semaphore_signal(barrier, inc=1, device_id=(x, peer // 4, peer % 4), device_id_type=MESH)
        return carry

    lax.fori_loop(1, 16, greet, 0)

    loads = [pltpu.make_async_copy(r.whole.at[i], r.w.at[i], r.load.at[i]) for i in range(4)]
    frames_in = r.rows_in.at[pl.ds(0, rows)]
    values = (r.q, r.k, r.v, r.o, r.p)
    early = [
        pltpu.make_async_copy(source, target, r.early.at[i])
        for i, (source, target) in enumerate(
            zip(
                (r.third_from, r.grad_from, r.rows_from, r.q1, r.k1, r.v1, r.o1, r.p1),
                (r.third, r.grad, frames_in) + values,
            )
        )
    ]
    kept = [
        pltpu.make_async_copy(source, target, r.keep.at[i])
        for i, (source, target) in enumerate(zip((r.q0, r.k0, r.v0, r.o0, r.p0), values))
    ]
    for copy in early[:2] + loads[2:] + early[2:] + loads[:2]:
        copy.start()
    spare = r.normed.shape[0] - rows
    for ref in (r.normed, r.branch, r.dk, r.dv):
        ref[rows:] = jnp.zeros((spare, ref.shape[1]), BF)
    r.total[rows:] = jnp.zeros((spare, model), F32)
    early[0].wait()
    early[1].wait()

    norm_into(r.third, r.norm.at[2], r.normed)
    flip_into(r.normed, r.normed_t)
    va = r.va.at[0]
    round_into(r.grad, r.branch, va, 8)
    flip_into(r.branch, r.branch_t)
    r.total[0:rows] = r.third[...] + r.db[...]
    r.gn[...] = jnp.zeros(r.gn.shape, F32)
    loads[2].wait()
    loads[3].wait()
    pl.semaphore_wait(barrier, 16)
    red = Reduction(r, where, x, y, k, z, r.own.shape[1], r.own.shape[2])
    size = r.ub.shape[2]
    halves = r.own.shape[2] // size

    def mlp(i, carry):
        t = (3 * i) % 4
        for half in range(halves):
            j = t * halves + half
            columns = pl.ds(pl.multiple_of(j * size, 128), size)
            up = r.w[2, :, columns]
            down = r.w[3, :, columns]
            hidden = nn(r.normed[...], up) + r.ub[j]
            cdf = 0.5 + 0.5 * lax.erf(hidden * (2.0**-0.5))
            active = (hidden * cdf).astype(BF)
            slope = cdf + hidden * (jnp.exp(-0.5 * hidden * hidden) * ((2.0 * jnp.pi) ** -0.5))
            rounded = (nn(r.branch[...], down) * slope).astype(BF)
            r.ups[j] = jnp.sum(rounded.astype(F32), axis=0, keepdims=True)
            r.total[...] += nt(active, down)
            r.gn[...] += nt(rounded, up)
            r.w[3, :, columns] = nn(r.branch_t[...], active).astype(BF)
            r.w[2, :, columns] = nn(r.normed_t[...], rounded).astype(BF)
        for s in (2 * i, 2 * i + 1):
            red.start(s)
        for s in (2 * i, 2 * i + 1):
            red.tick(s)
        return carry

    lax.fori_loop(0, 4, mlp, 0)

    by_frame(r.total.at[pl.ds(0, rows)], r.y_send, r.mix)
    outs = []
    for d in range(1, 4):
        peer = (c + d) % 4
        copy = pltpu.make_async_remote_copy(
            src_ref=r.y_send.at[pl.ds(peer * 4, 4)], dst_ref=r.y_home.at[c],
            send_sem=r.ys.at[d], recv_sem=r.yq.at[d], device_id=(x, peer, z), device_id_type=MESH,
        )
        copy.start()
        outs.append(copy)
    y_own = pltpu.make_async_copy(r.y_send.at[pl.ds(c * 4, 4)], r.y_home.at[c], r.ys.at[0])
    y_own.start()

    norm_back_into(r.third, r.norm.at[2], r.gn, r.grad, va, 6)
    for copy in early[2:]:
        copy.wait()
    loads[1].wait()
    for t in range(4):
        r.o[t, rows:] = jnp.zeros((spare, r.o.shape[2]), BF)
    group = TG * frames
    att = Attention(
        share // TG, group, None, r.w.at[1], None,
        *(ref.at[:, pl.ds(0, rows)] for ref in (r.q, r.k, r.v)), r.o, small_probs(r.p, group),
    )

    def each(first):
        def after(i):
            red.start(first + i)
            maybe(i > 0 if first == 12 else None, lambda: red.tick(first + i))

        return after

    attention_back(
        att, frames_in, r.grad, r.norm.at[1], r.normed, r.normed_t, r.branch, r.branch_t,
        r.dk, r.dv, r.gn, r.w.at[1], r.bias1, va, 3, each(8),
    )
    for copy in kept:
        copy.start()
    by_frame(r.grad, r.g_send, r.mix)

    def to_frame(d):
        peer = (me + d) % 16
        return pltpu.make_async_remote_copy(
            src_ref=r.g_send.at[peer], dst_ref=r.g_recv.at[me],
            send_sem=r.gs.at[d], recv_sem=r.gq.at[d], device_id=(x, peer // 4, peer % 4), device_id_type=MESH,
        )

    def go(d, carry):
        to_frame(d).start()
        return carry

    lax.fori_loop(1, 16, go, 0)
    r.g_recv[me] = r.g_send[me]
    red.tick(12)
    for copy in kept:
        copy.wait()
    loads[0].wait()
    srows = clips * SP
    for clip in range(clips):
        for zz in range(4):
            row = clip * SP + zz * home_places
            r.rows_in[row : row + home_places] = r.x[zz, clip].astype(F32)
        r.rows_in[pl.ds(clip * SP + places, SP - places)] = jnp.zeros((SP - places, model), F32)
        r.total[pl.ds(clip * SP + places, SP - places)] = jnp.zeros((SP - places, model), F32)

    def come(d, carry):
        to_frame(d).wait()
        return carry

    lax.fori_loop(1, 16, come, 0)
    for cc in range(4):
        for zz in range(4):
            r.third[0:share] = r.g_recv[cc * 4 + zz].astype(F32)
            for start, count, clip, place in pair_segments(cc, share, clips, home_places):
                row = clip * SP + zz * home_places + place
                r.total[row : row + count] = r.third[start : start + count]

    att = Attention(clips, SP, None, r.w.at[0], None, r.q, r.k, r.v, r.o, spatial_probs(r.p))
    attention_back(
        att, r.rows_in, r.total, r.norm.at[0], r.normed, r.normed_t, r.branch, r.branch_t, r.dk, r.dv, r.gn,
        r.w.at[0], r.bias0, va, 0, each(12),
    )
    for zz in range(4):
        for clip in range(clips):
            row = clip * SP + zz * home_places
            r.third[0:home_places] = r.total[row : row + home_places]
            r.home_send[zz, clip] = r.third[0:home_places].astype(BF)
    for d in range(1, 4):
        peer = (z + d) % 4
        copy = pltpu.make_async_remote_copy(
            src_ref=r.home_send.at[peer], dst_ref=r.g_home.at[z],
            send_sem=r.hs.at[d], recv_sem=r.hq.at[d], device_id=(x, c, peer), device_id_type=MESH,
        )
        copy.start()
        outs.append(copy)
    g_own = pltpu.make_async_copy(r.home_send.at[z], r.g_home.at[z], r.hs.at[0])
    g_own.start()

    for j in range(r.ups.shape[0]):
        va[9 + j // halves : 10 + j // halves, (j % halves) * size : (j % halves + 1) * size] = r.ups[j]
    for i, ref in enumerate((r.bias0, r.bias1)):
        for t in range(4):
            va[16 + i * 8 + t * 2 : 18 + i * 8 + t * 2, 0:256] = ref[t]
    sides = ("core", "x", "y", "z1", "z2")

    def v_copy(j):
        return red.remote(r.va.at[j], r.vr.at[j], r.vs.at[j], r.vq.at[j], sides[j])

    v_copy(0).start()

    def rest(n, carry):
        red.tick(n)
        for j in range(5):

            @pl.when(n == STEPS + j)
            def _():
                v_copy(j).wait()
                if j < 4:
                    r.va[j + 1] = r.va[j] + r.vr[j]
                    v_copy(j + 1).start()
                else:
                    r.vectors[...] = r.va[j] + r.vr[j]

        return carry

    lax.fori_loop(STEPS, STEPS + 13, rest, 0)
    red.finish()
    for copy in outs:
        copy.wait()
    y_own.wait()
    g_own.wait()


def backward(x, rows_in, third, grad, whole, kept, norm, up_bias, down_bias, own_rows, width, frames):
    _, clips, home_places, model = x.shape
    rows, srows = third.shape[0], clips * SP
    places, share = home_places * 4, rows // frames
    size = 384
    anywhere, vmem = pl.BlockSpec(memory_space=pl.ANY), pl.BlockSpec(memory_space=pltpu.VMEM)
    args = (x, rows_in, third, grad, whole, *kept, norm, up_bias.reshape(-1, 1, size), down_bias)
    in_specs = [vmem] + [anywhere] * 14 + [vmem] * 3
    sub = (own_rows, width)
    big = max(rows, srows)

    def v(*dims, dtype=BF):
        return pltpu.VMEM(dims, dtype)

    def f(*dims):
        return pltpu.VMEM(dims, F32)

    dma = pltpu.SemaphoreType.DMA
    scratch = (
        [v(*whole.shape)]
        + [v(4, big, 256)] * 4
        + [v(4, clips, 3 * SP, SP)]
        + [f(big, model), f(big, model), f(rows, model), f(rows, model), f(big, model)]
        + [f(model // 128, rows, 128)]
        + [v(big, model), v(model, big), v(big, model), v(model, big), v(big, 256), v(big, 256)]
        + [v(frames, share, model), v(frames, share, model), v(frames, share, model)]
        + [v(4, clips, places // 4, model), f(4, 2, 256), f(4, 2, 256), f(up_bias.shape[0] // size, 1, size)]
        + [v(STEPS, 2, 2, *sub)]
        + [v(STEPS, *sub)] * 4
        + [v(PIECES, *sub)]
        + [f(5, 32, model)] * 2
        + [dma((4,))]
        + [dma((STEPS, 2, 2))] * 2
        + [dma((STEPS,))] * 9
        + [dma((5,))] * 2
        + [dma((4,))] * 2
        + [dma((16,))] * 2
        + [dma((4,))] * 2
        + [dma((5,))]
        + [dma((8,))]
    )
    return pl.pallas_call(
        back_kernel,
        out_shape=(
            shape(4, frames // 4, share, model),
            shape(4, clips, places // 4, model),
            shape(PIECES, *sub, dtype=F32),
            shape(32, model, dtype=F32),
        ),
        in_specs=in_specs,
        out_specs=[anywhere, anywhere, vmem, vmem],
        scratch_shapes=scratch,
        compiler_params=pltpu.CompilerParams(
            collective_id=2, has_side_effects=True, vmem_limit_bytes=67043328
        ),
        name="backward",
    )(*args)


def local(
    inputs,
    cotangent,
    norm_gain,
    norm_bias,
    attn_weight,
    attn_bias,
    out_weight,
    out_bias,
    up_weight,
    up_bias,
    down_weight,
    down_bias,
):
    ranks_c = lax.axis_size("ctx")
    tp_rank = lax.axis_index("tp")
    clips, frames, places, model = inputs.shape
    width = attn_weight.shape[3]

    shard = jnp.concatenate(
        [
            jnp.concatenate(
                [
                    attn_weight.transpose(0, 2, 1, 3).reshape(2, attn_weight.shape[2], 3 * width),
                    out_weight.transpose(0, 2, 1),
                ],
                axis=2,
            ),
            up_weight[None],
            down_weight.T[None],
        ]
    )
    norm = jnp.stack([norm_gain, norm_bias], axis=1)

    pairs = clips * places
    share = -(-pairs // ranks_c)
    share += -share % TG

    def home_to_spatial(values):
        return lax.all_to_all(values, "tp", split_axis=1, concat_axis=2, tiled=True)

    def spatial_to_home(values):
        return lax.all_to_all(values, "tp", split_axis=2, concat_axis=1, tiled=True)

    def home_to_temporal(values):
        rows = values.transpose(1, 0, 2, 3).reshape(frames, pairs, model)
        rows = jnp.pad(rows, ((0, 0), (0, share * ranks_c - pairs), (0, 0)))
        return lax.all_to_all(rows, "ctx", split_axis=1, concat_axis=0, tiled=True)

    def temporal_to_home(values):
        rows = lax.all_to_all(values, "ctx", split_axis=0, concat_axis=1, tiled=True)[:, :pairs]
        return rows.reshape(frames, clips, places, model).transpose(1, 0, 2, 3)

    ups = up_bias.shape[0] // model
    bias = jnp.pad(attn_bias, ((0, 0), (0, 6), (0, 256 - width)))
    if lax.axis_size("fsdp") == 2 and (ranks_c, lax.axis_size("tp")) == (4, 4):
        frames *= ranks_c
        whole, first, *kept = forward(shard, bias, inputs, cotangent, norm, out_bias, frames, share)
        kept, rows = kept[5:10] + kept[:5], kept[10:]
        home, grad_home, own, vectors = backward(
            first, *rows, whole, kept, norm, up_bias, down_bias[None], attn_weight.shape[2] // 4, up_weight.shape[1], frames
        )
        frames //= ranks_c
        outputs = home.transpose(1, 0, 2, 3).reshape(frames, -1, model)[:, :pairs]
        outputs = outputs.reshape(frames, clips, places, model).transpose(1, 0, 2, 3)
        input_grad = grad_home.transpose(1, 0, 2, 3)
        sums = vectors[16:, :256].reshape(2, 4, 2, 256)[..., :width].transpose(0, 2, 1, 3)
        attn_bias_sums = sums.reshape(2, 2, model)
    else:
        whole, bias = gather(shard, bias)
        bias = bias[:, :, :2].transpose(1, 0, 2, 3)
        first = home_to_spatial(inputs)
        spatial_shape = first.shape
        first = first.reshape((-1,) + first.shape[2:])
        second, *kept = spatial_forward(first, whole, bias[0], norm[0], out_bias[0:1])
        second = home_to_temporal(spatial_to_home(second.reshape(spatial_shape)))
        grad_out = home_to_temporal(cotangent)
        result, grad_second, grad_attn1, grad_up, grad_down, bias1, vec1, vec2, grad_up_bias = temporal(
            second, grad_out, whole, bias[1], norm[1], norm[2], out_bias[1:2], up_bias, down_bias[None]
        )
        outputs = temporal_to_home(result)
        grad_second = home_to_spatial(temporal_to_home(grad_second)).reshape(first.shape)
        grad_first, grad_attn0, bias0, vec0 = spatial_back(first, grad_second, whole, norm[0], kept)
        input_grad = spatial_to_home(grad_first.reshape(spatial_shape))
        bias_sums = jnp.stack([bias0, bias1])[..., :width].transpose(0, 2, 1, 3)
        lines = [vec0, vec1, vec2, grad_up_bias, bias_sums]
        flat = jnp.concatenate([line.reshape(-1, model) for line in lines])
        vectors = jnp.pad(flat, ((0, -flat.shape[0] % 8), (0, 0)))
        own, vectors = scatter([grad_attn0, grad_attn1, grad_up, grad_down], vectors)
        attn_bias_sums = vectors[9 + ups : 13 + ups].reshape(2, 2, model)
    triples = vectors[:9].reshape(3, 3, model)
    attn = own[:2].reshape(2, own.shape[1], 4, width)
    return (
        outputs,
        input_grad,
        triples[:, 0],
        triples[:, 1],
        attn[:, :, :3].transpose(0, 2, 1, 3),
        lax.dynamic_slice_in_dim(attn_bias_sums, tp_rank * width, width, 2),
        attn[:, :, 3].transpose(0, 2, 1),
        triples[:2, 2],
        own[2],
        vectors[9 : 9 + ups].reshape(-1),
        own[3].T,
        triples[2, 2],
    )


def solution(mesh):
    return jax.shard_map(
        local,
        mesh=mesh,
        in_specs=(
            P("fsdp", "ctx", "tp", None),
            P("fsdp", "ctx", "tp", None),
            P(),
            P(),
            P(None, None, "fsdp", "tp"),
            P(None, None, "tp"),
            P(None, "tp", "fsdp"),
            P(),
            P("fsdp", "tp"),
            P(),
            P("tp", "fsdp"),
            P(),
        ),
        out_specs=(
            P("fsdp", "ctx", "tp", None),
            P("fsdp", "ctx", "tp", None),
            P(),
            P(),
            P(None, None, ("fsdp", "ctx"), "tp"),
            P(None, None, "tp"),
            P(None, "tp", ("fsdp", "ctx")),
            P(),
            P(("fsdp", "ctx"), "tp"),
            P(),
            P("tp", ("fsdp", "ctx")),
            P(),
        ),
        check_vma=False,
    )
```

profile of v0, /device:TPU:0, one launch (start us, length us, event | category | flops | bytes accessed | tf_op | source)
XLA Modules:
  0.0 305.2 jit_solution(13995103530475909576)
XLA Ops:
  0.6 0.0 copy-start.5
  0.7 0.0 copy-start.4
  0.7 0.8 stack.10
  1.5 0.7 stack.9
  2.2 0.6 pad_maximum_fusion.1.refs_4_.refs_15_
  2.8 1.5 copy.37
  4.3 1.3 copy.38
  5.6 0.0 copy-done.5
  5.6 0.2 copy.36
  5.8 0.0 copy-done.4
  5.8 0.0 copy-start.2
  5.9 0.0 copy-start.3
  5.9 1.7 pad_maximum_fusion.refs_0_
  7.6 0.0 copy-done.2
  7.6 0.0 copy-start.7
  7.6 0.9 copy.39.refs_2_
  8.6 0.0 copy-done.3
  8.6 0.9 copy.40.refs_3_
  9.5 0.7 compare_select_fusion.refs_6_
  10.3 0.0 copy-done.7
  10.3 0.6 pad.4.refs_1_
  10.9 125.4 %forward.1 = (bf16[4,768,3072]{2,1,0:T(8,128)(2,1)}, bf16[4,2,49,768]{3,2,1,0:T(8,128)(2,1)}, bf16[4,416,256]{2,1,0:T(8,128)(2,1)}, bf16[4,416,256]{2,1,0:T(8,12...) custom-call(bf16[4,384,768]{2,1,0:T(8,128)(2,1)} %pad_maximum_fusion, ...), custom_call_target="tpu_custom_call" | custom-call | tf_op jit(solution)/shard_map/forward/pallas_call | solution.py:972
  136.3 1.3 broadcast_in_dim.23.refs_17_
  137.6 155.9 %backward.1 = (bf16[4,4,25,768]{3,2,1,0:T(8,128)(2,1)}, bf16[4,2,49,768]{3,2,1,0:T(8,128)(2,1)}, f32[4,96,768]{2,1,0:T(8,128)}, f32[32,768]{1,0:T(8,128)}) custom-call(bf16[4,2,49,768]{3,2,1,0:T(8,128)(2,1)} %get-tuple-element.31.refs_0_, f32[400,768]{1,0:T(8,128)} %get-tuple-element.32.refs_1_, f32[400,768]{1,0:T(8,128)} %get-tuple-element.33.refs_2_, ...), custom_call_target="tpu_custom_call" | custom-call | tf_op jit(solution)/shard_map/backward/pallas_call | solution.py:1254
  293.5 0.0 copy-start.6
  293.5 0.0 copy-start.1
  293.5 1.2 slice.46
  294.7 0.6 reshape.141
  295.3 0.9 copy.58
  296.2 0.0 copy-done.6
  296.3 0.6 copy_bitcast_fusion.1
  296.9 0.0 copy-start
  296.9 0.2 slice.61
  297.1 0.8 copy.52
  297.9 0.0 copy-done.1
  297.9 0.5 copy.41
  298.4 1.0 slice.56
  299.4 2.2 copy.48
  301.7 0.0 copy-done
  301.7 0.8 slice_bitcast_fusion
  302.5 0.6 copy.59
  303.1 0.6 slice_reduce_fusion
  303.8 0.1 reshape.143
  303.9 0.7 constant_dynamic-slice_fusion
  304.5 0.6 reshape.144
  (11 shorter events, 0.1 us)
Async XLA Ops:
  0.6 5.0 %copy-start.5 = (bf16[2,192,384]{2,1,0:T(8,128)(2,1)S(1)}, bf16[2,192,384]{2,1,0:T(8,128)(2,1)}, u32[]{:S(2)}) copy-start(bf16[2,192,384]{2,1,0:T(8,128)(2,1)} %param.18) | copy-start | bytes 884740
  0.7 5.2 %copy-start.4 = (bf16[384,768]{1,0:T(8,128)(2,1)S(1)}, bf16[384,768]{1,0:T(8,128)(2,1)}, u32[]{:S(2)}) copy-start(bf16[384,768]{1,0:T(8,128)(2,1)} %param.20) | copy-start | bytes 1769476
  5.8 1.8 copy-start.2
  5.9 2.7 copy-start.3
  7.6 2.7 copy-start.7
  293.5 2.7 copy-start.6
  293.5 4.4 %copy-start.1 = (bf16[4,4,25,768]{3,2,1,0:T(8,128)(2,1)S(1)}, bf16[4,4,25,768]{3,2,1,0:T(8,128)(2,1)}, u32[]{:S(2)}) copy-start(bf16[4,4,25,768]{3,2,1,0:T(8,128)(2,1)} %get-tuple-element.46) | copy-start | bytes 1843204
  296.9 4.8 %copy-start = (f32[4,96,768]{2,1,0:T(8,128)S(1)}, f32[4,96,768]{2,1,0:T(8,128)}, u32[]{:S(2)}) copy-start(f32[4,96,768]{2,1,0:T(8,128)} %get-tuple-element.49) | copy-start | bytes 3538948
where the time goes:
time: 306 us; the launch traced here: 305 us
  Pallas kernels  281 us (92%)
  local copies, waits for them, and re-layouts  19.9 us (7%)
  other arithmetic  3.14 us (1%)
    pallas_call x1, Pallas kernels, backward(): pl.pallas_call(back_kernel, out_shape=(shape(4, frames // 4, share, model...  156 us
    pallas_call x1, Pallas kernels, forward(): pl.pallas_call(forward_kernel, out_shape=outs, in_specs=[vmem, vmem, anyw...  125 us
    unnamed x24, local copies, waits for them, and re-layouts  7.97 us

commit v1 on v0

--- a/solution.py
+++ b/solution.py
@@ -632,7 +632,8 @@
 
 
 STAGES = 7
-X_LAST = (3,)
+X_LAST = ()
+WIDE = (3,)
 FIRST = [[(0, 0), (1, 0)], [(0, 1)], [(0, 2), (1, 1)], [(0, 3), (1, 2), (2, 0), (0, 4), (1, 3), (3, 0), (0, 5), (1, 4), (2, 1), (0, 6)]]
 WITH_SPATIAL = [[(1, 5)], [(3, 1)], [(1, 6)], [(2, 2)]]
 WITH_EXCHANGE = [[(3, 2)], [(2, 3)], [(3, 3)]]
@@ -649,32 +650,46 @@
         c, other_y, last = self.c, (1 - y) * 2 + k, 3
         self.stages = [[] for _ in range(STAGES)]
 
-        def wait(stage, unit, when=None):
-            self.stages[stage].append(("wait", unit, when))
-
-        def send(stage, side, unit, when=None, mine=False, x_last=None):
-            entry = (side, unit, when, mine, x_last, len(self.sends))
+        def wait(stage, unit, when=None, use=None):
+            self.stages[stage].append(("wait", unit, when, use))
+
+        def send(stage, side, unit, when=None, mine=False, use=None):
+            entry = (side, unit, when, mine, use, len(self.sends))
             self.sends.append(entry)
             self.stages[stage].append(("send",) + entry)
 
-        me = (x, c, z)
+        def wide(piece):
+            return piece in WIDE
+
+        def narrow(piece):
+            return piece not in WIDE
+
+        def x_last(piece):
+            return piece in X_LAST
+
+        def y_last(piece):
+            return piece not in X_LAST
+
+        me, beside = (x, c, z), (x, other_y, z)
         send(0, "up", me, z < last, True)
         send(0, "down", me, z > 0, True)
         send(0, "x", me, None, True)
-        send(0, "x", (x, other_y, z), None, True)
+        send(0, "up", beside, z < last, True, wide)
+        send(0, "down", beside, z > 0, True, wide)
+        send(0, "x", beside, None, True)
         for d in (1, 2, 3):
             for sign in (-1, 1):
                 t = z + sign * d
                 have = (t >= 0) if sign < 0 else (t <= last)
-                unit = (x, c, t)
-                wait(d, unit, have)
-                if d < last:
-                    if sign < 0:
-                        send(d, "up", unit, have & (z < last))
-                    else:
-                        send(d, "down", unit, have & (z > 0))
+                for unit, use in (((x, c, t), None), ((x, other_y, t), wide)):
+                    wait(d, unit, have, use)
+                    if d < last:
+                        if sign < 0:
+                            send(d, "up", unit, have & (z < last), use=use)
+                        else:
+                            send(d, "down", unit, have & (z > 0), use=use)
                 for side in ("x", "y", "core"):
-                    send(d, side, unit, have)
+                    send(d, side, (x, c, t), have, use=narrow if side == "y" else None)
             if d == 1:
                 wait(1, (1 - x, c, z))
                 send(1, "core", (1 - x, c, z))
@@ -686,10 +701,10 @@
                 t = z + sign * d
                 have = (t >= 0) if sign < 0 else (t <= last)
                 wait(d + 1, (1 - x, c, t), have)
-                send(d + 1, "y", (1 - x, c, t), have, x_last=False)
+                send(d + 1, "y", (1 - x, c, t), have, use=y_last)
                 send(d + 1, "core", (1 - x, c, t), have)
-                wait(d + 1, (x, other_y, t), have)
-                send(d + 1, "x", (x, other_y, t), have, x_last=True)
+                wait(d + 1, (x, other_y, t), have, narrow)
+                send(d + 1, "x", (x, other_y, t), have, use=x_last)
                 send(d + 1, "core", (x, other_y, t), have)
                 wait(d + 2, (1 - x, other_y, t), have)
                 send(d + 2, "core", (1 - x, other_y, t), have)
@@ -703,9 +718,6 @@
         f, cc, t = unit
         row = pl.multiple_of((f * 4 + cc) * self.rows, 16)
         return self.r.w.at[piece, pl.ds(row, self.rows), pl.ds(pl.multiple_of(t * self.width, 128), self.width)]
-
-    def active(self, piece):
-        return lambda entry: entry[4] is None or entry[4] == (piece in X_LAST)
 
     def copy(self, piece, entry):
         side, unit, _, mine, _, number = entry
@@ -737,9 +749,10 @@
             self.own(piece).start()
         for kind, *rest in self.stages[number]:
             if kind == "wait":
-                unit, when = rest
-                maybe(when, lambda: self.arrived(piece, unit))
-            elif self.active(piece)(rest):
+                unit, when, use = rest
+                if use is None or use(piece):
+                    maybe(when, lambda: self.arrived(piece, unit))
+            elif rest[4] is None or rest[4](piece):
                 maybe(rest[2], lambda: self.copy(piece, rest).start())
         if number == STAGES - 1:
             self.own(piece).wait()
@@ -768,7 +781,7 @@
         lax.fori_loop(0, PIECES, body, 0)
         for piece in range(PIECES):
             for entry in self.sends:
-                if entry[4] is not None and self.active(piece)(entry):
+                if entry[4] is not None and entry[4](piece):
                     maybe(entry[2], lambda: self.copy(piece, entry).wait_send())
 
 
@@ -956,7 +969,7 @@
     outs = [shape(*whole), shape(*blocks)] + [shape(*size) for size in attention * 2]
     outs += [shape(rows, model, dtype=F32)] * 3
     dma = pltpu.SemaphoreType.DMA
-    sends = 58
+    sends = 68
     scratch = (
         [pltpu.VMEM(whole, BF), pltpu.VMEM((4,) + bias.shape, F32)]
         + [pltpu.VMEM(size, BF) for size in attention]

time: 306 us -> 305 us (level)
    pallas_call x1, Pallas kernels: 156 us -> 150 us  [backward(): pl.pallas_call(back_kernel, out_shape=(shape(4, frames // 4, share, model...]
    pallas_call x1, Pallas kernels: 125 us -> 131 us  [forward(): pl.pallas_call(forward_kernel, out_shape=outs, in_specs=[vmem, vmem, anyw...]
where the time goes in v1:
time: 305 us
  Pallas kernels  281 us (92%)
  local copies, waits for them, and re-layouts  19.9 us (7%)
  other arithmetic  3.14 us (1%)
    pallas_call x1, Pallas kernels, backward(): pl.pallas_call(back_kernel, out_shape=(shape(4, frames // 4, share, model...  150 us
    pallas_call x1, Pallas kernels, forward(): pl.pallas_call(forward_kernel, out_shape=outs, in_specs=[vmem, vmem, anyw...  131 us
    unnamed x24, local copies, waits for them, and re-layouts  7.97 us

profile of v1, /device:TPU:0, one launch (start us, length us, event | category | flops | bytes accessed | tf_op | source)
XLA Modules:
  0.0 304.7 jit_solution(16647003378758600095)
XLA Ops:
  0.6 0.0 copy-start.5
  0.7 0.0 copy-start.4
  0.7 0.8 stack.10
  1.5 0.7 stack.9
  2.2 0.6 pad_maximum_fusion.1.refs_4_.refs_15_
  2.8 1.5 copy.37
  4.3 1.3 copy.38
  5.6 0.0 copy-done.5
  5.6 0.2 copy.36
  5.8 0.0 copy-done.4
  5.8 0.0 copy-start.2
  5.9 0.0 copy-start.3
  5.9 1.7 pad_maximum_fusion.refs_0_
  7.6 0.0 copy-done.2
  7.6 0.0 copy-start.7
  7.6 0.9 copy.39.refs_2_
  8.6 0.0 copy-done.3
  8.6 0.9 copy.40.refs_3_
  9.5 0.7 compare_select_fusion.refs_6_
  10.3 0.0 copy-done.7
  10.3 0.6 pad.4.refs_1_
  10.9 131.3 %forward.1 = (bf16[4,768,3072]{2,1,0:T(8,128)(2,1)}, bf16[4,2,49,768]{3,2,1,0:T(8,128)(2,1)}, bf16[4,416,256]{2,1,0:T(8,128)(2,1)}, bf16[4,416,256]{2,1,0:T(8,12...) custom-call(bf16[4,384,768]{2,1,0:T(8,128)(2,1)} %pad_maximum_fusion, ...), custom_call_target="tpu_custom_call" | custom-call | tf_op jit(solution)/shard_map/forward/pallas_call | solution.py:985
  142.2 1.3 broadcast_in_dim.23.refs_17_
  143.5 149.6 %backward.1 = (bf16[4,4,25,768]{3,2,1,0:T(8,128)(2,1)}, bf16[4,2,49,768]{3,2,1,0:T(8,128)(2,1)}, f32[4,96,768]{2,1,0:T(8,128)}, f32[32,768]{1,0:T(8,128)}) custom-call(bf16[4,2,49,768]{3,2,1,0:T(8,128)(2,1)} %get-tuple-element.31.refs_0_, f32[400,768]{1,0:T(8,128)} %get-tuple-element.32.refs_1_, f32[400,768]{1,0:T(8,128)} %get-tuple-element.33.refs_2_, ...), custom_call_target="tpu_custom_call" | custom-call | tf_op jit(solution)/shard_map/backward/pallas_call | solution.py:1267
  293.1 0.0 copy-start.6
  293.1 0.0 copy-start.1
  293.1 1.2 slice.46
  294.3 0.6 reshape.141
  294.8 0.9 copy.58
  295.8 0.0 copy-done.6
  295.8 0.6 copy_bitcast_fusion.1
  296.4 0.0 copy-start
  296.4 0.2 slice.61
  296.6 0.8 copy.52
  297.5 0.0 copy-done.1
  297.5 0.5 copy.41
  298.0 1.0 slice.56
  299.0 2.2 copy.48
  301.2 0.0 copy-done
  301.2 0.8 slice_bitcast_fusion
  302.1 0.6 copy.59
  302.7 0.6 slice_reduce_fusion
  303.3 0.1 reshape.143
  303.4 0.7 constant_dynamic-slice_fusion
  304.1 0.6 reshape.144
  (11 shorter events, 0.1 us)
Async XLA Ops:
  0.6 5.0 %copy-start.5 = (bf16[2,192,384]{2,1,0:T(8,128)(2,1)S(1)}, bf16[2,192,384]{2,1,0:T(8,128)(2,1)}, u32[]{:S(2)}) copy-start(bf16[2,192,384]{2,1,0:T(8,128)(2,1)} %param.18) | copy-start | bytes 884740
  0.7 5.2 %copy-start.4 = (bf16[384,768]{1,0:T(8,128)(2,1)S(1)}, bf16[384,768]{1,0:T(8,128)(2,1)}, u32[]{:S(2)}) copy-start(bf16[384,768]{1,0:T(8,128)(2,1)} %param.20) | copy-start | bytes 1769476
  5.8 1.8 copy-start.2
  5.9 2.7 copy-start.3
  7.6 2.7 copy-start.7
  293.1 2.7 copy-start.6
  293.1 4.4 %copy-start.1 = (bf16[4,4,25,768]{3,2,1,0:T(8,128)(2,1)S(1)}, bf16[4,4,25,768]{3,2,1,0:T(8,128)(2,1)}, u32[]{:S(2)}) copy-start(bf16[4,4,25,768]{3,2,1,0:T(8,128)(2,1)} %get-tuple-element.46) | copy-start | bytes 1843204
  296.4 4.8 %copy-start = (f32[4,96,768]{2,1,0:T(8,128)S(1)}, f32[4,96,768]{2,1,0:T(8,128)}, u32[]{:S(2)}) copy-start(f32[4,96,768]{2,1,0:T(8,128)} %get-tuple-element.49) | copy-start | bytes 3538948
